TPU v7x, 128 devices: a whole 4x4x4 slice. The times are simulated.
128 devices in a mesh: node: 8 (over y_lo, z), bond: 16 (over y_hi, x, core).
Axes of the slice: x: 4, y: 4 (y_hi: 2, y_lo: 2; y = y_hi * 2 + y_lo), z: 4, core: 2. Of those that a mesh axis runs over, the one named last changes fastest.
Arguments:
- bottom_nodes: float32 [8, 128, 128, 128], P('node', 'bond'), may hold values from -0.046875 to 0.046875
- upper_nodes: float32 [8, 128, 128, 128], P(None, 'bond', 'node'), may hold values from -0.046875 to 0.046875
- leaf_up: float32 [8, 3, 2, 128, 128], P('node'), may hold values from -2 to 3
- outside_env: float32 [3, 128, 128], replicated, may hold values from -2 to 3
- top_env: float32 [3, 128, 128], replicated, may hold values from -2 to 3
Outputs:
- leaf_down: float32 [8, 3, 2, 128, 128], P('node', None, None, 'bond')
- subtree_env: float32 [3, 128, 128], replicated
All inputs are finite; a program needn't handle non-finite values.
Results may differ from a plain program's by a relative error of at most 0.0001.
Values sent between devices are 32-bit elements; how exact they have to be, the bound alone decides.
No kernel may reach another device: no remote copies, remote signals or barrier semaphores. Data moves between devices by JAX's collectives and lax.ppermute only.
A program may use at most 128 MiB of HBM per device.

v0:
```python
import jax
import jax.numpy as jnp
from jax import lax
from jax.sharding import Mesh, PartitionSpec as P

NODE = ("ylo", "zhi", "zlo")
BOND = ("yhi", "x", "core")
SLOT_OF = (4, 2, 5, 1, 6, 3, 7, 0)


def ein(spec, a, b):
    return jnp.einsum(spec, a, b, precision=lax.Precision.HIGHEST)


def after(x, other):
    return lax.optimization_barrier((x, other))[0]


def swap_cores(half, core, axis):
    other = lax.ppermute(half, "core", [(0, 1), (1, 0)])
    low = jnp.where(core == 0, half, other)
    high = jnp.where(core == 0, other, half)
    return jnp.concatenate([low, high], axis=axis)


def up_rows(tensor, rows, left_env, right_env):
    middle = ein("pab,ac->pcb", rows, left_env)
    product = ein("pcb,bd->pcd", middle, right_env)
    return ein("pcd,qcd->pq", product, tensor)


def halves(tensor, core, axis):
    size = tensor.shape[axis] // 2
    return lax.dynamic_slice_in_dim(tensor, core * size, size, axis=axis)


def local(bottom_nodes, upper_nodes, leaf_up, outside_env, top_env):
    group = lax.axis_index(NODE)
    bond = lax.axis_index(BOND)
    core = lax.axis_index("core")
    op = jnp.minimum(lax.axis_index("x"), 2)
    width = bottom_nodes.shape[2]
    rows = bottom_nodes.shape[1]
    parts = width // rows
    send = jnp.stack([upper_nodes[s] for s in SLOT_OF])
    got = lax.all_to_all(send, NODE, 0, 0, tiled=True)
    shard = jnp.moveaxis(got, 0, 1).reshape(rows, width, width)
    upper = lax.all_gather(shard, BOND, axis=0, tiled=True)
    mine = bottom_nodes[0]
    left_leaf = leaf_up[0, :, 0]
    right_leaf = leaf_up[0, :, 1]
    middle = ein("kac,pcd->kpad", left_leaf, after(mine, shard))
    product = ein("kpad,kbd->kpab", middle, right_leaf)
    both = jnp.concatenate([mine[None], product])
    both = jnp.moveaxis(both.reshape(4, rows, parts, rows, width), 2, 0)
    both = lax.all_to_all(both, BOND, 0, 0, tiled=True)
    both = jnp.moveaxis(both, 1, 0).reshape(4, width, rows, width)
    mine_a = both[0]
    gram = ein("pab,kqab->kpq", mine_a, both[1:])
    pieces = jnp.moveaxis(gram.reshape(3, parts, rows, width), 1, 0)
    pieces = lax.all_to_all(pieces, BOND, 0, 0, tiled=True)
    env = jnp.sum(pieces, axis=0)
    by_x = jnp.stack([env[0], env[1], env[2], env[2]])
    by_dest = jnp.broadcast_to(by_x[None, None, :, None], (2, 2, 4, 2, rows, width))
    by_dest = by_dest.reshape(2 * parts, rows, width)
    pair = lax.all_to_all(by_dest, ("zlo",) + BOND, 0, 0, tiled=True)
    left3, right3 = pair.reshape(2, width, width)

    def move(x, *pairs):
        return lax.ppermute(x, NODE, pairs)

    upper_rows = halves(upper, core, 0)
    up2 = up_rows(upper, upper_rows, left3, right3)
    ends = jnp.stack([move(up2, (0, 1), (4, 5)), move(up2, (2, 1), (6, 5))])
    left2, right2 = swap_cores(ends, core, 1)
    up1 = up_rows(upper, upper_rows, left2, right2)
    ends = jnp.stack([move(up1, (1, 3)), move(up1, (5, 3))])
    left1, right1 = swap_cores(ends, core, 1)
    upper_a = halves(upper, core, 1)
    upper_b = halves(upper, core, 2)

    def first_row(right_env):
        return ein("pab,bd->pad", upper_a, right_env)

    def second_row(left_env):
        return ein("pab,ac->pcb", upper_b, left_env)

    def worked_by(above):
        return ein("pq,qcd->pcd", above, upper)

    def first_of(row, worked):
        return ein("pad,pcd->ac", row, worked)

    def second_of(row, worked):
        return ein("pcb,pcd->bd", row, worked)

    top = lax.dynamic_index_in_dim(top_env, op, 0, keepdims=False)
    outside = lax.dynamic_index_in_dim(outside_env, op, 0, keepdims=False)
    crown = first_of(first_row(outside), worked_by(top))
    above = swap_cores(move(crown, (7, 3)), core, 0)
    worked = worked_by(above)
    first = first_of(first_row(right1), worked)
    second = second_of(second_row(left1), worked)
    root = up_rows(upper, upper_rows, left1, right1)
    above = swap_cores(move(first, (3, 1)) + move(second, (3, 5)), core, 0)
    worked = worked_by(above)
    first = first_of(first_row(right2), worked)
    second = second_of(second_row(left2), worked)
    above = move(first, (1, 0), (5, 4)) + move(second, (1, 2), (5, 6))
    above = swap_cores(above, core, 0)
    worked = worked_by(above)
    first = first_of(first_row(right3), worked)
    second = second_of(second_row(left3), worked)
    sent = move(second, (0, 1), (2, 3), (4, 5), (6, 7))
    last = jnp.where(group % 2 == 0, first, sent)
    root = jnp.where(group == 3, root, 0.0)
    root = root + move(root, (3, 7))
    root = root + move(root, (3, 1), (7, 5))
    root = root + move(root, (3, 2), (1, 0), (7, 6), (5, 4))
    ends = lax.all_gather(jnp.stack([last, root]), "x", axis=0, tiled=False)
    ends = swap_cores(ends[:3], core, 2)
    above = ends[:, 0]
    root_env = ends[:, 1]
    whole = lax.all_gather(after(mine, upper), BOND, axis=0, tiled=True)
    row = ein("pab,kbd->kpad", mine_a, right_leaf)
    grown = ein("kpq,kpad->kqad", above, row)
    first = ein("kqad,qcd->kac", grown, whole)
    turned = lax.dynamic_slice_in_dim(jnp.swapaxes(whole, 1, 2), bond * rows, rows, axis=1)
    row = ein("pba,kac->kbpc", turned, left_leaf)
    grown = ein("kpq,kbpc->kbqc", above, row)
    second = ein("kbqc,qcd->kbd", grown, whole)
    leaf_down = jnp.stack([first, second], 1)[None]
    return (leaf_down, root_env)


def solution(mesh):
    shape = (2, 2, 2, 2, 4, 2)
    fine = Mesh(mesh.devices.reshape(shape), NODE + BOND)
    placed = (
        P(NODE, BOND, None, None),
        P(None, BOND, NODE, None),
        P(NODE, None, None, None, None),
        P(),
        P(),
    )
    return jax.shard_map(
        local,
        mesh=fine,
        in_specs=placed,
        out_specs=(P(NODE, None, None, BOND, None), P()),
        check_vma=False,
    )
```

profile of v0, /device:TPU:67, one launch (start us, length us, event | category | flops | bytes accessed | tf_op | source)
XLA Modules:
  0.0 506.2 jit_solution(13400908433034332693)
XLA Ops:
  14.1 12.1 %all_to_all.20 = f32[8,8,16,128]{3,2,1,0:T(8,128)S(1)} all-to-all(f32[8,8,16,128]{3,2,1,0:T(8,128)S(1)} %slice_dynamic-update-slice_fusion), channel_id=1, replica_groups=mesh['ylo'=2,'zhi'=2,'zlo'=2,'yhi'=2,'x'=4,'core'=2] {'ylo','zhi','zlo'}, dimensions={0} | all-to-all | bytes 1048576 | tf_op jit(solution)/shard_map/all_to_all | solution.py:46
  31.7 40.8 %all_to_all.21 = f32[16,4,8,8,128]{4,3,2,1,0:T(8,128)S(1)} all-to-all(f32[16,4,8,8,128]{4,3,2,1,0:T(8,128)S(1)} %copy_bitcast_fusion.2), channel_id=1, replica_groups=mesh['ylo'=2,'zhi'=2,'zlo'=2,'yhi'=2,'x'=4,'core'=2] {'yhi','x','core'}, dimensions={0} | all-to-all | bytes 4194304 | tf_op jit(solution)/shard_map/all_to_all | solution.py:56
  94.4 36.1 %all-gather.4.cloned.1.call-done = f32[128,128,128]{2,0,1:T(8,128)} async-done(((f32[8,128,128]{2,0,1:T(8,128)}), f32[128,128,128]{2,0,1:T(8,128)}) %all-gather.4.cloned.1.call-update) | async-done | bytes 8388624 | tf_op jit(solution)/shard_map/all_gather | solution.py:48
  135.4 8.7 %fusion.26 = f32[128,64,128]{2,0,1:T(8,128)S(1)} fusion(f32[64,128,128]{2,0,1:T(8,128)} %constant_dynamic-slice_fusion.1, f32[32,8,128]{2,1,0:T(8,128)S(1)} %all-to-all-done.3), kind=kOutput, calls=%fused_computation.26 | convolution fusion | flops 1610612736 | bytes 8454144 | tf_op jit(solution)/shard_map/pab,ac->pcb/dot_general | solution.py:12
  150.5 9.0 %convolution_bitcast_fusion.6 = f32[64,128]{1,0:T(8,128)S(1)} fusion(f32[64,128,128]{2,0,1:T(8,128)S(1)} %fusion.14, f32[128,128,128]{2,0,1:T(8,128)S(1)} %bitcast.242), kind=kOutput, calls=%fused_computation.59 | convolution fusion | flops 1610612736 | bytes 12615680 | tf_op jit(solution)/shard_map/pcd,qcd->pq/dot_general | solution.py:12
  175.3 9.4 %copy.46 = f32[128,128,128]{1,0,2:T(8,128)} copy(f32[128,128,128]{2,0,1:T(8,128)} %all-gather.4.cloned.1.call-done) | data formatting | bytes 16777216 | tf_op jit(solution)/shard_map/all_gather | solution.py:48
  184.7 10.9 %fusion.101 = f32[128,128,128]{1,0,2:T(8,128)S(1)} fusion(f32[128,128,128]{1,0,2:T(8,128)} %copy.46, f32[3,128,128]{2,1,0:T(8,128)S(1)} %copy-done, s32[]{:T(128)S(6)} %select_n.104), kind=kOutput, calls=%fused_computation.118 | convolution fusion | flops 3221225472 | bytes 16842756 | tf_op jit(solution)/shard_map/pq,qcd->pcd/dot_general | solution.py:12
  201.5 8.9 %constant_dynamic-slice_fusion = f32[128,128,64]{2,0,1:T(8,128)} fusion(f32[128,128,128]{2,0,1:T(8,128)} %all-gather.4.cloned.1.call-done, s32[]{:T(128)S(6)} %select_n.97), kind=kLoop, calls=%fused_computation.152 | loop fusion | bytes 8388612 | tf_op jit(solution)/shard_map/dynamic_slice | solution.py:34
  219.3 11.8 %fusion.92 = f32[128,128,128]{2,0,1:T(8,128)} fusion(f32[128,128,128]{2,0,1:T(8,128)} %all-gather.4.cloned.1.call-done, f32[64,128]{1,0:T(8,128)S(1)} %get-tuple-element.21, f32[64,128]{1,0:T(8,128)S(1)} %get-tuple-element.20), kind=kOutput, calls=%fused_computation.106 | convolution fusion | flops 3221241856 | bytes 16842752 | tf_op jit(solution)/shard_map/pq,qcd->pcd/dot_general | solution.py:12
  231.1 9.4 %copy.27 = f32[128,128,128]{1,0,2:T(8,128)} copy(f32[128,128,128]{2,0,1:T(8,128)} %fusion.92) | data formatting | bytes 16777216 | tf_op jit(solution)/shard_map/pq,qcd->pcd/dot_general | solution.py:12
  240.5 8.8 %fusion.24 = f32[128,64,128]{2,0,1:T(8,128)S(1)} fusion(f32[64,128,128]{2,0,1:T(8,128)} %constant_dynamic-slice_fusion.1, f32[2,64,128]{2,1,0:T(8,128)S(1)} %get-tuple-element.15, f32[2,64,128]{2,1,0:T(8,128)S(1)} %get-tuple-element.14), kind=kOutput, calls=%fused_computation.24 | convolution fusion | flops 1610629120 | bytes 8519680 | tf_op jit(solution)/shard_map/pab,ac->pcb/dot_general | solution.py:12
  255.6 9.2 %convolution_bitcast_fusion.5 = f32[64,128]{1,0:T(8,128)S(1)} fusion(f32[64,128,128]{2,0,1:T(8,128)S(1)} %fusion.12, f32[128,128,128]{2,0,1:T(8,128)S(1)} %bitcast.244), kind=kOutput, calls=%fused_computation.58 | convolution fusion | flops 1610612736 | bytes 12615680 | tf_op jit(solution)/shard_map/pcd,qcd->pq/dot_general | solution.py:12
  287.7 11.0 %fusion.45 = f32[64,128]{1,0:T(8,128)S(1)} fusion(f32[128,128,128]{2,0,1:T(8,128)} %fusion.92, f32[128,128,64]{1,0,2:T(8,128)S(1)} %fusion.111), kind=kOutput, calls=%fused_computation.47 | convolution fusion | flops 1610612736 | bytes 12615680 | tf_op jit(solution)/shard_map/pcb,pcd->bd/dot_general | solution.py:12
  309.9 8.3 %convolution_bitcast_fusion.3 = f32[64,128]{1,0:T(8,128)S(1)} fusion(f32[128,64,128]{0,1,2:T(8,128)} %copy.44, f32[128,128,128]{1,0,2:T(8,128)} %copy.27), kind=kOutput, calls=%fused_computation.56 | convolution fusion | flops 1610612736 | bytes 12615680 | tf_op jit(solution)/shard_map/pad,pcd->ac/dot_general | solution.py:12
  332.2 8.8 %fusion.54 = f32[64,128]{1,0:T(8,128)S(1)} fusion(f32[64,128,128]{2,0,1:T(8,128)S(1)} %fusion.4, f32[128,128,128]{2,0,1:T(8,128)S(1)} %bitcast.248, pred[]{:T(512)S(6)} %eq.9), kind=kOutput, calls=%fused_computation.51 | convolution fusion | flops 1610620928 | bytes 12615681 | tf_op jit(solution)/shard_map/pcd,qcd->pq/dot_general | solution.py:12
  342.5 9.5 %fusion.95 = f32[128,128,128]{2,0,1:T(8,128)} fusion(f32[128,128,128]{2,0,1:T(8,128)S(1)} %bitcast.248, f32[64,128]{1,0:T(8,128)S(1)} %get-tuple-element.19, f32[64,128]{1,0:T(8,128)S(1)} %get-tuple-element.18), kind=kOutput, calls=%fused_computation.110 | convolution fusion | flops 3221241856 | bytes 16842752 | tf_op jit(solution)/shard_map/pq,qcd->pcd/dot_general | solution.py:12
  352.0 9.4 %copy.28 = f32[128,128,128]{1,0,2:T(8,128)} copy(f32[128,128,128]{2,0,1:T(8,128)} %fusion.95) | data formatting | bytes 16777216 | tf_op jit(solution)/shard_map/pq,qcd->pcd/dot_general | solution.py:12
  361.4 10.7 %fusion.48 = f32[64,128]{1,0:T(8,128)S(1)} fusion(f32[128,128,128]{2,0,1:T(8,128)} %fusion.95, f32[128,128,64]{1,0,2:T(8,128)} %fusion.107), kind=kOutput, calls=%fused_computation.48 | convolution fusion | flops 1610612736 | bytes 12615680 | tf_op jit(solution)/shard_map/pcb,pcd->bd/dot_general | solution.py:12
  399.7 10.5 %fusion.98 = f32[128,128,128]{2,0,1:T(8,128)S(1)} fusion(f32[128,128,128]{2,0,1:T(8,128)} %all-gather.4.cloned.1.call-done, f32[64,128]{1,0:T(8,128)S(1)} %get-tuple-element.17, f32[64,128]{1,0:T(8,128)S(1)} %get-tuple-element.16), kind=kOutput, calls=%fused_computation.114 | convolution fusion | flops 3221241856 | bytes 16842752 | tf_op jit(solution)/shard_map/pq,qcd->pcd/dot_general | solution.py:12
  417.6 9.0 %collective-permute-start.14 = (f32[64,128]{1,0:T(8,128)S(1)}, f32[64,128]{1,0:T(8,128)S(1)}, u32[]{:S(2)}, u32[]{:S(2)}) collective-permute-start(f32[64,128]{1,0:T(8,128)S(1)} %fusion.51), channel_id=1, source_target_pairs={{0,16},{32,48},{64,80},{96,112},{1,17},{33,49},{65,81},{97,113},{2... | collective-permute-start | bytes 98312 | tf_op jit(solution)/shard_map/ppermute | solution.py:70
  426.7 9.4 %copy.29 = f32[128,128,128]{1,0,2:T(8,128)} copy(f32[128,128,128]{2,0,1:T(8,128)} %copy-done.2) | data formatting | bytes 16777216 | tf_op jit(solution)/shard_map/pq,qcd->pcd/dot_general | solution.py:12
  436.1 8.2 %fusion.56 = f32[1,64,128]{2,1,0:T(8,128)S(1)} fusion(f32[64,128]{1,0:T(8,128)S(1)} %collective-permute-done.14, f32[128,64,128]{0,1,2:T(8,128)} %copy.39, f32[128,128,128]{1,0,2:T(8,128)} %copy.29, pred[]{:T(512)S(6)} %eq.8), kind=kOutput, calls=%fused_computation.54 | convolution fusion | flops 1610620928 | bytes 12648449 | tf_op jit(solution)/shard_map/pad,pcd->ac/dot_general | solution.py:12
  444.3 9.0 %all-gather = f32[8,64,128]{2,1,0:T(8,128)S(1)} all-gather(f32[2,64,128]{2,1,0:T(8,128)S(1)} %pad_maximum_fusion.5), channel_id=2, replica_groups=mesh['ylo'=2,'zhi'=2,'zlo'=2,'yhi'=2,'x'=4,'core'=2] {'x'}, dimensions={0}, use_global_device_ids=true | all-gather | bytes 327680 | tf_op jit(solution)/shard_map/all_gather | solution.py:120
  475.4 9.6 %copy.33 = f32[128,128,128]{2,0,1:T(8,128)} copy(f32[128,128,128]{1,0,2:T(8,128)} %all-gather.6.cloned.1.call-done) | data formatting | bytes 16777216 | tf_op jit(solution)/shard_map/all_gather | solution.py:124
  (167 shorter events, 202.8 us)
Async XLA Ops:
  7.2 177.6 %copy-start = (f32[3,128,128]{2,1,0:T(8,128)S(1)}, f32[3,128,128]{2,1,0:T(8,128)}, u32[]{:S(2)}) copy-start(f32[3,128,128]{2,1,0:T(8,128)} %param.9) | copy-start | bytes 589828
  7.2 123.3 %all-gather.4.cloned.1.call-start = ((), (), s32[]{:S(2)}) async-start(), calls=%async_computation.4 | async-start | bytes 8912896 | tf_op jit(solution)/shard_map/all_gather | solution.py:48
  75.1 13.2 %all-to-all-start.2 = ((f32[16,3,8,128]{3,2,1,0:T(8,128)}), f32[16,3,8,128]{3,2,1,0:T(8,128)S(1)}, u32[]{:S(2)}, u32[]{:S(2)}) async-start(f32[16,3,8,128]{3,2,1,0:T(8,128)} %bitcast.240), calls=%async_computation.2 | async-start | bytes 393216 | tf_op jit(solution)/shard_map/all_to_all | solution.py:61
  89.1 46.3 %all-to-all-start.3 = ((f32[32,8,128]{2,1,0:T(8,128)}), f32[32,8,128]{2,1,0:T(8,128)S(1)}, u32[]{:S(2)}, u32[]{:S(2)}) async-start(f32[32,8,128]{2,1,0:T(8,128)} %bitcast.22), calls=%async_computation.3 | async-start | bytes 262144 | tf_op jit(solution)/shard_map/all_to_all | solution.py:66
  94.3 372.3 %all-gather.6.cloned.1.call-start = ((), (), s32[]{:S(2)}) async-start(), calls=%async_computation.5 | async-start | bytes 8912896 | tf_op jit(solution)/shard_map/all_gather | solution.py:124
  159.5 59.0 %collective-permute-start = (f32[64,128]{1,0:T(8,128)S(1)}, f32[64,128]{1,0:T(8,128)S(1)}, u32[]{:S(2)}, u32[]{:S(2)}) collective-permute-start(f32[64,128]{1,0:T(8,128)S(1)} %convolution_bitcast_fusion.6), channel_id=1, source_target_pairs={{0,16},{64,80},{1,17},{65,81},{2,18},{66,82},{3,19},{67,83},{4,20}... | collective-permute-start | bytes 98312 | tf_op jit(solution)/shard_map/ppermute | solution.py:70
  160.1 58.3 %collective-permute-start.1 = (f32[64,128]{1,0:T(8,128)S(1)}, f32[64,128]{1,0:T(8,128)S(1)}, u32[]{:S(2)}, u32[]{:S(2)}) collective-permute-start(f32[64,128]{1,0:T(8,128)S(1)} %convolution_bitcast_fusion.6), channel_id=1, source_target_pairs={{32,16},{96,80},{33,17},{97,81},{34,18},{98,82},{35,19},{99,83},{3... | collective-permute-start | bytes 98312 | tf_op jit(solution)/shard_map/ppermute | solution.py:70
  200.9 17.0 %collective-permute-start.6 = (f32[64,128]{1,0:T(8,128)S(1)}, f32[64,128]{1,0:T(8,128)S(1)}, u32[]{:S(2)}, u32[]{:S(2)}) collective-permute-start(f32[64,128]{1,0:T(8,128)S(1)} %convolution_bitcast_fusion.4), channel_id=1, source_target_pairs={{112,48},{113,49},{114,50},{115,51},{116,52},{117,53},{118,54},{11... | collective-permute-start | bytes 98312 | tf_op jit(solution)/shard_map/ppermute | solution.py:70
  217.8 1.4 collective-permute-start.7
  218.4 22.0 %collective-permute-start.2 = (f32[2,64,128]{2,1,0:T(8,128)S(1)}, f32[2,64,128]{2,1,0:T(8,128)S(1)}, u32[]{:S(2)}, u32[]{:S(2)}) collective-permute-start(f32[2,64,128]{2,1,0:T(8,128)S(1)} %pad_maximum_fusion.3), channel_id=1, source_target_pairs={{0,1},{1,0},{2,3},{3,2},{4,5},{5,4},{6,7},{7,6},{8,9},{9,8},{10,11... | collective-permute-start | bytes 196616 | tf_op jit(solution)/shard_map/ppermute | solution.py:20
  264.9 6.5 %collective-permute-start.3 = (f32[64,128]{1,0:T(8,128)S(1)}, f32[64,128]{1,0:T(8,128)S(1)}, u32[]{:S(2)}, u32[]{:S(2)}) collective-permute-start(f32[64,128]{1,0:T(8,128)S(1)} %convolution_bitcast_fusion.5), channel_id=1, source_target_pairs={{16,48},{17,49},{18,50},{19,51},{20,52},{21,53},{22,54},{23,55},{2... | collective-permute-start | bytes 98312 | tf_op jit(solution)/shard_map/ppermute | solution.py:70
  265.5 5.8 %collective-permute-start.4 = (f32[64,128]{1,0:T(8,128)S(1)}, f32[64,128]{1,0:T(8,128)S(1)}, u32[]{:S(2)}, u32[]{:S(2)}) collective-permute-start(f32[64,128]{1,0:T(8,128)S(1)} %convolution_bitcast_fusion.5), channel_id=1, source_target_pairs={{80,48},{81,49},{82,50},{83,51},{84,52},{85,53},{86,54},{87,55},{8... | collective-permute-start | bytes 98312 | tf_op jit(solution)/shard_map/ppermute | solution.py:70
  271.4 10.7 %collective-permute-start.5 = (f32[2,64,128]{2,1,0:T(8,128)S(1)}, f32[2,64,128]{2,1,0:T(8,128)S(1)}, u32[]{:S(2)}, u32[]{:S(2)}) collective-permute-start(f32[2,64,128]{2,1,0:T(8,128)S(1)} %pad_maximum_fusion.4), channel_id=1, source_target_pairs={{0,1},{1,0},{2,3},{3,2},{4,5},{5,4},{6,7},{7,6},{8,9},{9,8},{10,11... | collective-permute-start | bytes 196616 | tf_op jit(solution)/shard_map/ppermute | solution.py:20
  298.7 33.2 %collective-permute-start.9 = (f32[64,128]{1,0:T(8,128)S(1)}, f32[64,128]{1,0:T(8,128)S(1)}, u32[]{:S(2)}, u32[]{:S(2)}) collective-permute-start(f32[64,128]{1,0:T(8,128)S(1)} %fusion.45), channel_id=1, source_target_pairs={{48,80},{49,81},{50,82},{51,83},{52,84},{53,85},{54,86},{55,87},{5... | collective-permute-start | bytes 98312 | tf_op jit(solution)/shard_map/ppermute | solution.py:70
  318.2 13.8 %collective-permute-start.8 = (f32[64,128]{1,0:T(8,128)S(1)}, f32[64,128]{1,0:T(8,128)S(1)}, u32[]{:S(2)}, u32[]{:S(2)}) collective-permute-start(f32[64,128]{1,0:T(8,128)S(1)} %convolution_bitcast_fusion.3), channel_id=1, source_target_pairs={{48,16},{49,17},{50,18},{51,19},{52,20},{53,21},{54,22},{55,23},{5... | collective-permute-start | bytes 98312 | tf_op jit(solution)/shard_map/ppermute | solution.py:70
  332.0 10.5 %collective-permute-start.10 = (f32[64,128]{1,0:T(8,128)S(1)}, f32[64,128]{1,0:T(8,128)S(1)}, u32[]{:S(2)}, u32[]{:S(2)}) collective-permute-start(f32[64,128]{1,0:T(8,128)S(1)} %add.49), channel_id=1, source_target_pairs={{0,1},{1,0},{2,3},{3,2},{4,5},{5,4},{6,7},{7,6},{8,9},{9,8},{10,11... | collective-permute-start | bytes 98312 | tf_op jit(solution)/shard_map/ppermute | solution.py:20
  341.0 45.6 %collective-permute-start.15 = (f32[64,128]{1,0:T(8,128)S(1)}, f32[64,128]{1,0:T(8,128)S(1)}, u32[]{:S(2)}, u32[]{:S(2)}) collective-permute-start(f32[64,128]{1,0:T(8,128)S(1)} %fusion.54), channel_id=1, source_target_pairs={{48,112},{49,113},{50,114},{51,115},{52,116},{53,117},{54,118},{55... | collective-permute-start | bytes 98312 | tf_op jit(solution)/shard_map/ppermute | solution.py:70
  372.1 15.2 %collective-permute-start.12 = (f32[64,128]{1,0:T(8,128)S(1)}, f32[64,128]{1,0:T(8,128)S(1)}, u32[]{:S(2)}, u32[]{:S(2)}) collective-permute-start(f32[64,128]{1,0:T(8,128)S(1)} %fusion.48), channel_id=1, source_target_pairs={{16,32},{80,96},{17,33},{81,97},{18,34},{82,98},{19,35},{83,99},{2... | collective-permute-start | bytes 98312 | tf_op jit(solution)/shard_map/ppermute | solution.py:70
  380.8 6.6 %collective-permute-start.11 = (f32[64,128]{1,0:T(8,128)S(1)}, f32[64,128]{1,0:T(8,128)S(1)}, u32[]{:S(2)}, u32[]{:S(2)}) collective-permute-start(f32[64,128]{1,0:T(8,128)S(1)} %convolution_bitcast_fusion.2), channel_id=1, source_target_pairs={{16,0},{80,64},{17,1},{81,65},{18,2},{82,66},{19,3},{83,67},{20,4}... | collective-permute-start | bytes 98312 | tf_op jit(solution)/shard_map/ppermute | solution.py:70
  386.7 11.3 %collective-permute-start.16 = (f32[64,128]{1,0:T(8,128)S(1)}, f32[64,128]{1,0:T(8,128)S(1)}, u32[]{:S(2)}, u32[]{:S(2)}) collective-permute-start(f32[64,128]{1,0:T(8,128)S(1)} %add.51), channel_id=1, source_target_pairs={{48,16},{112,80},{49,17},{113,81},{50,18},{114,82},{51,19},{115,83... | collective-permute-start | bytes 98312 | tf_op jit(solution)/shard_map/ppermute | solution.py:70
  387.4 12.3 %collective-permute-start.13 = (f32[64,128]{1,0:T(8,128)S(1)}, f32[64,128]{1,0:T(8,128)S(1)}, u32[]{:S(2)}, u32[]{:S(2)}) collective-permute-start(f32[64,128]{1,0:T(8,128)S(1)} %add.50), channel_id=1, source_target_pairs={{0,1},{1,0},{2,3},{3,2},{4,5},{5,4},{6,7},{7,6},{8,9},{9,8},{10,11... | collective-permute-start | bytes 98312 | tf_op jit(solution)/shard_map/ppermute | solution.py:20
  397.9 28.7 %collective-permute-start.17 = (f32[64,128]{1,0:T(8,128)S(1)}, f32[64,128]{1,0:T(8,128)S(1)}, u32[]{:S(2)}, u32[]{:S(2)}) collective-permute-start(f32[64,128]{1,0:T(8,128)S(1)} %add.52), channel_id=1, source_target_pairs={{48,32},{16,0},{112,96},{80,64},{49,33},{17,1},{113,97},{81,65},{5... | collective-permute-start | bytes 98312 | tf_op jit(solution)/shard_map/ppermute | solution.py:70
  417.6 18.5 %collective-permute-start.14 = (f32[64,128]{1,0:T(8,128)S(1)}, f32[64,128]{1,0:T(8,128)S(1)}, u32[]{:S(2)}, u32[]{:S(2)}) collective-permute-start(f32[64,128]{1,0:T(8,128)S(1)} %fusion.51), channel_id=1, source_target_pairs={{0,16},{32,48},{64,80},{96,112},{1,17},{33,49},{65,81},{97,113},{2... | collective-permute-start | bytes 98312 | tf_op jit(solution)/shard_map/ppermute | solution.py:70
  453.3 8.6 %collective-permute-start.18 = (f32[3,2,64,128]{3,2,0,1:T(8,128)S(1)}, f32[3,2,64,128]{3,2,0,1:T(8,128)S(1)}, u32[]{:S(2)}, u32[]{:S(2)}) collective-permute-start(f32[3,2,64,128]{3,2,0,1:T(8,128)S(1)} %copy.31), channel_id=1, source_target_pairs={{0,1},{1,0},{2,3},{3,2},{4,5},{5,4},{6,7},{7,6},{8,9},{9,8},{10,11... | collective-permute-start | bytes 589832 | tf_op jit(solution)/shard_map/ppermute | solution.py:20
  (22 other events, 254.9 us)
Sparse Core Ops, SparseCore 0:
  27.3 103.1 all-gather.3
  132.7 76.9 all-gather.5
where the time goes:
time: 516 us; the launch traced here: 506 us
  matrix products  236 us (46%)
  local copies, waits for them, and re-layouts  108 us (21%)
  blocking collectives  61.9 us (12%)
  waiting for transfers between devices  44.2 us (9%)
  starting transfers between devices  39.6 us (8%)
  between operations  15.1 us (3%)
    dot_general x36, matrix products, ein(): return jnp.einsum(spec, a, b, precision=lax.Precision.HIGHEST)  236 us
    dot_general x9, local copies, waits for them, and re-layouts, ein(): return jnp.einsum(spec, a, b, precision=lax.Precision.HIGHEST)  52 us
    all_to_all x1, blocking collectives, local(): both = lax.all_to_all(both, BOND, 0, 0, tiled=True)  40.8 us
    all_gather x1, waiting for transfers between devices, local(): upper = lax.all_gather(shard, BOND, axis=0, tiled=True)  36.1 us
    ppermute x13, starting transfers between devices, move(): return lax.ppermute(x, NODE, pairs)  23.1 us
    dynamic_slice x3, local copies, waits for them, and re-layouts, halves(): return lax.dynamic_slice_in_dim(tensor, core * size, size, axis=axis)  21.2 us
    all_to_all x1, blocking collectives, local(): got = lax.all_to_all(send, NODE, 0, 0, tiled=True)  12.1 us
  transfers between devices with their start and end apart: 23, of which 3 were waited for; matrix products, arithmetic and copies ran while one was open for 60% of the time, Pallas kernels for 0%

commit v1 on v0

--- a/solution.py
+++ b/solution.py
@@ -45,7 +45,9 @@
     send = jnp.stack([upper_nodes[s] for s in SLOT_OF])
     got = lax.all_to_all(send, NODE, 0, 0, tiled=True)
     shard = jnp.moveaxis(got, 0, 1).reshape(rows, width, width)
-    upper = lax.all_gather(shard, BOND, axis=0, tiled=True)
+    upper = jnp.concatenate(
+        lax.all_to_all(jnp.stack([shard] * lax.axis_size(BOND)), BOND, 0, 0), axis=0
+    )
     mine = bottom_nodes[0]
     left_leaf = leaf_up[0, :, 0]
     right_leaf = leaf_up[0, :, 1]

time: 516 us -> 604 us (1.17)
  waiting for transfers between devices: 44.2 us -> 148 us
  blocking collectives: 61.9 us -> 9.22 us
  starting transfers between devices: 39.6 us -> 60.5 us
  matrix products: 236 us -> 246 us
    all_to_all x0 -> x3, waiting for transfers between devices: none -> 141 us  [the longest x1 113 us: local(): lax.all_to_all(jnp.stack([shard] * lax.axis_size(BOND)), BOND, 0, 0)]
    all_to_all x2 -> x0, blocking collectives: 52.9 us -> none  [the longest x1 40.8 us: local(): both = lax.all_to_all(both, BOND, 0, 0, tiled=True)]
    all_gather x1 -> x0, waiting for transfers between devices: 36.1 us -> none  [local(): upper = lax.all_gather(shard, BOND, axis=0, tiled=True)]
    all_to_all x0 -> x3, starting transfers between devices: none -> 18.4 us  [the longest x1 7.76 us: local(): both = lax.all_to_all(both, BOND, 0, 0, tiled=True)]
    dot_general x36, matrix products: 236 us -> 246 us  [ein(): return jnp.einsum(spec, a, b, precision=lax.Precision.HIGHEST)]
    reshape x0 -> x1, local copies, waits for them, and re-layouts: none -> 9.43 us  [local(): jnp.concatenate(lax.all_to_all(jnp.stack([shard] * lax.axis_size(BOND)),...]
    all_gather x1 -> x0, local copies, waits for them, and re-layouts: 9.41 us -> none  [local(): upper = lax.all_gather(shard, BOND, axis=0, tiled=True)]
    all_to_all x0 -> x2, local copies, waits for them, and re-layouts: none -> 7.89 us  [the longest x1 7.86 us: local(): lax.all_to_all(jnp.stack([shard] * lax.axis_size(BOND)), BOND, 0, 0)]
  transfers between devices with their start and end apart: 23 -> 25, of which waited for: 3 -> 5; matrix products, arithmetic and copies ran while one was open for 60% -> 54% of each run, Pallas kernels for 0% -> 0%
where the time goes in v1:
time: 604 us; the launch traced here: 596 us
  matrix products  246 us (41%)
  waiting for transfers between devices  148 us (25%)
  local copies, waits for them, and re-layouts  113 us (19%)
  starting transfers between devices  60.5 us (10%)
  between operations  15.2 us (3%)
  blocking collectives  9.22 us (2%)
    dot_general x36, matrix products, ein(): return jnp.einsum(spec, a, b, precision=lax.Precision.HIGHEST)  246 us
    all_to_all x1, waiting for transfers between devices, local(): lax.all_to_all(jnp.stack([shard] * lax.axis_size(BOND)), BOND, 0, 0)  113 us
    dot_general x7, local copies, waits for them, and re-layouts, ein(): return jnp.einsum(spec, a, b, precision=lax.Precision.HIGHEST)  49.8 us
    all_to_all x1, waiting for transfers between devices, local(): both = lax.all_to_all(both, BOND, 0, 0, tiled=True)  23.3 us
    dynamic_slice x3, local copies, waits for them, and re-layouts, halves(): return lax.dynamic_slice_in_dim(tensor, core * size, size, axis=axis)  22.6 us
    ppermute x13, starting transfers between devices, move(): return lax.ppermute(x, NODE, pairs)  22 us
  transfers between devices with their start and end apart: 25, of which 5 were waited for; matrix products, arithmetic and copies ran while one was open for 54% of the time, Pallas kernels for 0%

profile of v1, /device:TPU:67, one launch (start us, length us, event | category | flops | bytes accessed | tf_op | source)
XLA Modules:
  0.0 596.0 jit_solution(7710201897402056958)
XLA Ops:
  29.1 23.3 %all-to-all-done.2 = f32[16,4,8,8,128]{4,3,2,1,0:T(8,128)S(1)} async-done(((f32[16,4,8,8,128]{4,3,2,1,0:T(8,128)}), f32[16,4,8,8,128]{4,3,2,1,0:T(8,128)S(1)}, u32[]{:S(2)}, u32[]{:S(2)}) %all-to-all-start.2) | async-done | bytes 2097184 | tf_op jit(solution)/shard_map/all_to_all | solution.py:58
  88.2 113.1 %all-to-all-done.1 = f32[16,8,128,128]{3,1,2,0:T(8,128)} async-done(((f32[16,8,128,128]{3,1,2,0:T(8,128)}), f32[16,8,128,128]{3,1,2,0:T(8,128)}, u32[]{:S(2)}, u32[]{:S(2)}) %all-to-all-start.1) | async-done | bytes 8388640 | tf_op jit(solution)/shard_map/all_to_all | solution.py:49
  221.8 8.4 %fusion.30 = f32[64,128,128]{2,1,0:T(8,128)S(1)} fusion(f32[64,128,128]{2,0,1:T(8,128)} %constant_dynamic-slice_fusion.1, f32[32,8,128]{2,1,0:T(8,128)S(1)} %all-to-all-done.4), kind=kOutput, calls=%fused_computation.31 | convolution fusion | flops 1610612736 | bytes 8454144 | tf_op jit(solution)/shard_map/pab,ac->pcb/dot_general | solution.py:12
  236.5 11.3 %convolution_bitcast_fusion.11 = f32[64,128]{1,0:T(8,128)S(1)} fusion(f32[64,128,128]{2,0,1:T(8,128)S(1)} %fusion.14, f32[16,8,128,128]{3,1,2,0:T(8,128)} %all-to-all-done.1), kind=kOutput, calls=%fused_computation.60 | convolution fusion | flops 1610612736 | bytes 12615680 | tf_op jit(solution)/shard_map/pcd,qcd->pq/dot_general | solution.py:12
  252.2 9.4 %copy.99 = f32[128,128,128]{1,0,2:T(8,128)} copy(f32[128,128,128]{2,0,1:T(8,128)} %bitcast.242) | data formatting | bytes 16777216 | tf_op jit(solution)/shard_map/reshape | solution.py:48
  273.6 10.7 %fusion.103 = f32[128,128,128]{1,0,2:T(8,128)S(1)} fusion(f32[128,128,128]{1,0,2:T(8,128)} %copy.99, f32[3,128,128]{2,1,0:T(8,128)S(1)} %copy-done, s32[]{:T(128)S(6)} %select_n.104), kind=kOutput, calls=%fused_computation.118 | convolution fusion | flops 3221225472 | bytes 16842756 | tf_op jit(solution)/shard_map/pq,qcd->pcd/dot_general | solution.py:12
  290.2 8.9 %constant_dynamic-slice_fusion = f32[128,128,64]{2,0,1:T(8,128)} fusion(f32[128,128,128]{2,0,1:T(8,128)} %bitcast.244, s32[]{:T(128)S(6)} %select_n.97), kind=kLoop, calls=%fused_computation.149 | loop fusion | bytes 8388612 | tf_op jit(solution)/shard_map/dynamic_slice | solution.py:34
  299.1 8.9 %copy.104 = f32[128,128,64]{1,0,2:T(8,128)} copy(f32[128,128,64]{2,0,1:T(8,128)} %constant_dynamic-slice_fusion) | data formatting | bytes 8388608 | tf_op jit(solution)/shard_map/dynamic_slice | solution.py:34
  309.8 12.0 %fusion.94 = f32[128,128,128]{2,0,1:T(8,128)} fusion(f32[64,128]{1,0:T(8,128)S(1)} %get-tuple-element.23, f32[64,128]{1,0:T(8,128)S(1)} %get-tuple-element.22, f32[16,8,128,128]{3,1,2,0:T(8,128)} %all-to-all-done.1), kind=kOutput, calls=%fused_computation.106 | convolution fusion | flops 3221241856 | bytes 16842752 | tf_op jit(solution)/shard_map/pq,qcd->pcd/dot_general | solution.py:12
  321.9 9.4 %copy.102 = f32[128,128,128]{1,0,2:T(8,128)} copy(f32[128,128,128]{2,0,1:T(8,128)} %fusion.94) | data formatting | bytes 16777216 | tf_op jit(solution)/shard_map/pq,qcd->pcd/dot_general | solution.py:12
  331.3 8.6 %fusion.33 = f32[64,128,128]{2,1,0:T(8,128)S(1)} fusion(f32[64,128,128]{2,0,1:T(8,128)} %constant_dynamic-slice_fusion.1, f32[2,64,128]{2,1,0:T(8,128)S(1)} %get-tuple-element.17, f32[2,64,128]{2,1,0:T(8,128)S(1)} %get-tuple-element.16), kind=kOutput, calls=%fused_computation.32 | convolution fusion | flops 1610629120 | bytes 8519680 | tf_op jit(solution)/shard_map/pab,ac->pcb/dot_general | solution.py:12
  346.3 11.3 %convolution_bitcast_fusion.10 = f32[64,128]{1,0:T(8,128)S(1)} fusion(f32[64,128,128]{2,0,1:T(8,128)S(1)} %fusion.12, f32[16,8,128,128]{3,1,2,0:T(8,128)} %all-to-all-done.1), kind=kOutput, calls=%fused_computation.59 | convolution fusion | flops 1610612736 | bytes 12615680 | tf_op jit(solution)/shard_map/pcd,qcd->pq/dot_general | solution.py:12
  381.0 11.0 %fusion.48 = f32[64,128]{1,0:T(8,128)S(1)} fusion(f32[128,128,128]{2,0,1:T(8,128)} %fusion.94, f32[128,128,64]{0,1,2:T(8,128)S(1)} %convolution_bitcast_fusion.2), kind=kOutput, calls=%fused_computation.48 | convolution fusion | flops 1610612736 | bytes 12615680 | tf_op jit(solution)/shard_map/pcb,pcd->bd/dot_general | solution.py:12
  403.1 8.3 %convolution_bitcast_fusion.8 = f32[64,128]{1,0:T(8,128)S(1)} fusion(f32[128,64,128]{0,1,2:T(8,128)} %copy.101, f32[128,128,128]{1,0,2:T(8,128)} %copy.102), kind=kOutput, calls=%fused_computation.57 | convolution fusion | flops 1610612736 | bytes 12615680 | tf_op jit(solution)/shard_map/pad,pcd->ac/dot_general | solution.py:12
  425.5 11.1 %fusion.57 = f32[64,128]{1,0:T(8,128)S(1)} fusion(f32[64,128,128]{2,0,1:T(8,128)S(1)} %fusion.4, pred[]{:T(512)S(6)} %eq.9, f32[16,8,128,128]{3,1,2,0:T(8,128)} %all-to-all-done.1), kind=kOutput, calls=%fused_computation.52 | convolution fusion | flops 1610620928 | bytes 12615681 | tf_op jit(solution)/shard_map/pcd,qcd->pq/dot_general | solution.py:12
  437.3 11.6 %fusion.97 = f32[128,128,128]{2,0,1:T(8,128)} fusion(f32[64,128]{1,0:T(8,128)S(1)} %get-tuple-element.21, f32[64,128]{1,0:T(8,128)S(1)} %get-tuple-element.20, f32[16,8,128,128]{3,1,2,0:T(8,128)} %all-to-all-done.1), kind=kOutput, calls=%fused_computation.110 | convolution fusion | flops 3221241856 | bytes 16842752 | tf_op jit(solution)/shard_map/pq,qcd->pcd/dot_general | solution.py:12
  448.9 9.4 %copy.107 = f32[128,128,128]{1,0,2:T(8,128)} copy(f32[128,128,128]{2,0,1:T(8,128)} %fusion.97) | data formatting | bytes 16777216 | tf_op jit(solution)/shard_map/pq,qcd->pcd/dot_general | solution.py:12
  458.3 10.7 %fusion.51 = f32[64,128]{1,0:T(8,128)S(1)} fusion(f32[128,128,128]{2,0,1:T(8,128)} %fusion.97, f32[128,128,64]{0,1,2:T(8,128)} %convolution_bitcast_fusion.1), kind=kOutput, calls=%fused_computation.49 | convolution fusion | flops 1610612736 | bytes 12615680 | tf_op jit(solution)/shard_map/pcb,pcd->bd/dot_general | solution.py:12
  496.6 10.5 %fusion.100 = f32[128,128,128]{2,0,1:T(8,128)S(1)} fusion(f32[64,128]{1,0:T(8,128)S(1)} %get-tuple-element.19, f32[64,128]{1,0:T(8,128)S(1)} %get-tuple-element.18, f32[16,8,128,128]{3,1,2,0:T(8,128)} %all-to-all-done.1), kind=kOutput, calls=%fused_computation.114 | convolution fusion | flops 3221241856 | bytes 16842752 | tf_op jit(solution)/shard_map/pq,qcd->pcd/dot_general | solution.py:12
  514.6 9.2 %collective-permute-start.14 = (f32[64,128]{1,0:T(8,128)S(1)}, f32[64,128]{1,0:T(8,128)S(1)}, u32[]{:S(2)}, u32[]{:S(2)}) collective-permute-start(f32[64,128]{1,0:T(8,128)S(1)} %fusion.54), channel_id=1, source_target_pairs={{0,16},{32,48},{64,80},{96,112},{1,17},{33,49},{65,81},{97,113},{2... | collective-permute-start | bytes 98312 | tf_op jit(solution)/shard_map/ppermute | solution.py:72
  523.8 9.4 %copy.112 = f32[128,128,128]{1,0,2:T(8,128)} copy(f32[128,128,128]{2,0,1:T(8,128)} %copy-done.2) | data formatting | bytes 16777216 | tf_op jit(solution)/shard_map/pq,qcd->pcd/dot_general | solution.py:12
  533.2 8.2 %fusion.59 = f32[1,64,128]{2,1,0:T(8,128)S(1)} fusion(f32[64,128]{1,0:T(8,128)S(1)} %collective-permute-done.14, f32[128,64,128]{0,1,2:T(8,128)} %copy.111, f32[128,128,128]{1,0,2:T(8,128)} %copy.112, pred[]{:T(512)S(6)} %eq.8), kind=kOutput, calls=%fused_computation.55 | convolution fusion | flops 1610620928 | bytes 12648449 | tf_op jit(solution)/shard_map/pad,pcd->ac/dot_general | solution.py:12
  541.4 9.2 %all-gather = f32[8,64,128]{2,1,0:T(8,128)S(1)} all-gather(f32[2,64,128]{2,1,0:T(8,128)S(1)} %pad_maximum_fusion.5), channel_id=2, replica_groups=mesh['ylo'=2,'zhi'=2,'zlo'=2,'yhi'=2,'x'=4,'core'=2] {'x'}, dimensions={0}, use_global_device_ids=true | all-gather | bytes 327680 | tf_op jit(solution)/shard_map/all_gather | solution.py:122
  565.3 9.4 %copy.124 = f32[128,128,128]{2,0,1:T(8,128)} copy(f32[128,128,128]{1,0,2:T(8,128)} %all-gather.3.cloned.1.call-done) | data formatting | bytes 16777216 | tf_op jit(solution)/shard_map/all_gather | solution.py:126
  (167 shorter events, 227.5 us)
Async XLA Ops:
  16.3 36.1 %all-to-all-start.2 = ((f32[16,4,8,8,128]{4,3,2,1,0:T(8,128)}), f32[16,4,8,8,128]{4,3,2,1,0:T(8,128)S(1)}, u32[]{:S(2)}, u32[]{:S(2)}) async-start(f32[16,4,8,8,128]{4,3,2,1,0:T(8,128)} %copy_bitcast_fusion.1), calls=%async_computation.2 | async-start | bytes 4194304 | tf_op jit(solution)/shard_map/all_to_all | solution.py:58
  52.4 11.4 %all-to-all-start = ((f32[8,8,16,128]{3,2,1,0:T(8,128)}), f32[8,8,16,128]{3,2,1,0:T(8,128)S(1)}, u32[]{:S(2)}, u32[]{:S(2)}) async-start(f32[8,8,16,128]{3,2,1,0:T(8,128)} %slice_dynamic-update-slice_fusion), calls=%async_computation | async-start | bytes 1048576 | tf_op jit(solution)/shard_map/all_to_all | solution.py:46
  63.9 14.1 %all-to-all-start.3 = ((f32[16,3,8,128]{3,2,1,0:T(8,128)}), f32[16,3,8,128]{3,2,1,0:T(8,128)S(1)}, u32[]{:S(2)}, u32[]{:S(2)}) async-start(f32[16,3,8,128]{3,2,1,0:T(8,128)} %bitcast.240), calls=%async_computation.3 | async-start | bytes 393216 | tf_op jit(solution)/shard_map/all_to_all | solution.py:63
  82.1 119.2 %all-to-all-start.1 = ((f32[16,8,128,128]{3,1,2,0:T(8,128)}), f32[16,8,128,128]{3,1,2,0:T(8,128)}, u32[]{:S(2)}, u32[]{:S(2)}) async-start(f32[16,8,128,128]{3,1,2,0:T(8,128)} %stack.47), calls=%async_computation.1 | async-start | bytes 16777216 | tf_op jit(solution)/shard_map/all_to_all | solution.py:49
  202.0 19.8 %all-to-all-start.4 = ((f32[32,8,128]{2,1,0:T(8,128)}), f32[32,8,128]{2,1,0:T(8,128)S(1)}, u32[]{:S(2)}, u32[]{:S(2)}) async-start(f32[32,8,128]{2,1,0:T(8,128)} %bitcast.23), calls=%async_computation.4 | async-start | bytes 262144 | tf_op jit(solution)/shard_map/all_to_all | solution.py:68
  208.5 352.3 %all-gather.3.cloned.1.call-start = ((), (), s32[]{:S(2)}) async-start(), calls=%async_computation.5 | async-start | bytes 8912896 | tf_op jit(solution)/shard_map/all_gather | solution.py:126
  247.8 61.2 %collective-permute-start = (f32[64,128]{1,0:T(8,128)S(1)}, f32[64,128]{1,0:T(8,128)S(1)}, u32[]{:S(2)}, u32[]{:S(2)}) collective-permute-start(f32[64,128]{1,0:T(8,128)S(1)} %convolution_bitcast_fusion.11), channel_id=1, source_target_pairs={{0,16},{64,80},{1,17},{65,81},{2,18},{66,82},{3,19},{67,83},{4,20}... | collective-permute-start | bytes 98312 | tf_op jit(solution)/shard_map/ppermute | solution.py:72
  248.5 60.5 %collective-permute-start.1 = (f32[64,128]{1,0:T(8,128)S(1)}, f32[64,128]{1,0:T(8,128)S(1)}, u32[]{:S(2)}, u32[]{:S(2)}) collective-permute-start(f32[64,128]{1,0:T(8,128)S(1)} %convolution_bitcast_fusion.11), channel_id=1, source_target_pairs={{32,16},{96,80},{33,17},{97,81},{34,18},{98,82},{35,19},{99,83},{3... | collective-permute-start | bytes 98312 | tf_op jit(solution)/shard_map/ppermute | solution.py:72
  289.6 18.4 %collective-permute-start.6 = (f32[64,128]{1,0:T(8,128)S(1)}, f32[64,128]{1,0:T(8,128)S(1)}, u32[]{:S(2)}, u32[]{:S(2)}) collective-permute-start(f32[64,128]{1,0:T(8,128)S(1)} %convolution_bitcast_fusion.9), channel_id=1, source_target_pairs={{112,48},{113,49},{114,50},{115,51},{116,52},{117,53},{118,54},{11... | collective-permute-start | bytes 98312 | tf_op jit(solution)/shard_map/ppermute | solution.py:72
  309.0 22.3 %collective-permute-start.2 = (f32[2,64,128]{2,1,0:T(8,128)S(1)}, f32[2,64,128]{2,1,0:T(8,128)S(1)}, u32[]{:S(2)}, u32[]{:S(2)}) collective-permute-start(f32[2,64,128]{2,1,0:T(8,128)S(1)} %pad_maximum_fusion.3), channel_id=1, source_target_pairs={{0,1},{1,0},{2,3},{3,2},{4,5},{5,4},{6,7},{7,6},{8,9},{9,8},{10,11... | collective-permute-start | bytes 196616 | tf_op jit(solution)/shard_map/ppermute | solution.py:20
  357.6 7.0 %collective-permute-start.3 = (f32[64,128]{1,0:T(8,128)S(1)}, f32[64,128]{1,0:T(8,128)S(1)}, u32[]{:S(2)}, u32[]{:S(2)}) collective-permute-start(f32[64,128]{1,0:T(8,128)S(1)} %convolution_bitcast_fusion.10), channel_id=1, source_target_pairs={{16,48},{17,49},{18,50},{19,51},{20,52},{21,53},{22,54},{23,55},{2... | collective-permute-start | bytes 98312 | tf_op jit(solution)/shard_map/ppermute | solution.py:72
  358.2 6.3 %collective-permute-start.4 = (f32[64,128]{1,0:T(8,128)S(1)}, f32[64,128]{1,0:T(8,128)S(1)}, u32[]{:S(2)}, u32[]{:S(2)}) collective-permute-start(f32[64,128]{1,0:T(8,128)S(1)} %convolution_bitcast_fusion.10), channel_id=1, source_target_pairs={{80,48},{81,49},{82,50},{83,51},{84,52},{85,53},{86,54},{87,55},{8... | collective-permute-start | bytes 98312 | tf_op jit(solution)/shard_map/ppermute | solution.py:72
  364.6 10.8 %collective-permute-start.5 = (f32[2,64,128]{2,1,0:T(8,128)S(1)}, f32[2,64,128]{2,1,0:T(8,128)S(1)}, u32[]{:S(2)}, u32[]{:S(2)}) collective-permute-start(f32[2,64,128]{2,1,0:T(8,128)S(1)} %pad_maximum_fusion.4), channel_id=1, source_target_pairs={{0,1},{1,0},{2,3},{3,2},{4,5},{5,4},{6,7},{7,6},{8,9},{9,8},{10,11... | collective-permute-start | bytes 196616 | tf_op jit(solution)/shard_map/ppermute | solution.py:20
  392.0 33.2 %collective-permute-start.9 = (f32[64,128]{1,0:T(8,128)S(1)}, f32[64,128]{1,0:T(8,128)S(1)}, u32[]{:S(2)}, u32[]{:S(2)}) collective-permute-start(f32[64,128]{1,0:T(8,128)S(1)} %fusion.48), channel_id=1, source_target_pairs={{48,80},{49,81},{50,82},{51,83},{52,84},{53,85},{54,86},{55,87},{5... | collective-permute-start | bytes 98312 | tf_op jit(solution)/shard_map/ppermute | solution.py:72
  411.4 13.8 %collective-permute-start.8 = (f32[64,128]{1,0:T(8,128)S(1)}, f32[64,128]{1,0:T(8,128)S(1)}, u32[]{:S(2)}, u32[]{:S(2)}) collective-permute-start(f32[64,128]{1,0:T(8,128)S(1)} %convolution_bitcast_fusion.8), channel_id=1, source_target_pairs={{48,16},{49,17},{50,18},{51,19},{52,20},{53,21},{54,22},{55,23},{5... | collective-permute-start | bytes 98312 | tf_op jit(solution)/shard_map/ppermute | solution.py:72
  425.2 12.1 %collective-permute-start.10 = (f32[64,128]{1,0:T(8,128)S(1)}, f32[64,128]{1,0:T(8,128)S(1)}, u32[]{:S(2)}, u32[]{:S(2)}) collective-permute-start(f32[64,128]{1,0:T(8,128)S(1)} %add.49), channel_id=1, source_target_pairs={{0,1},{1,0},{2,3},{3,2},{4,5},{5,4},{6,7},{7,6},{8,9},{9,8},{10,11... | collective-permute-start | bytes 98312 | tf_op jit(solution)/shard_map/ppermute | solution.py:20
  436.6 47.1 %collective-permute-start.15 = (f32[64,128]{1,0:T(8,128)S(1)}, f32[64,128]{1,0:T(8,128)S(1)}, u32[]{:S(2)}, u32[]{:S(2)}) collective-permute-start(f32[64,128]{1,0:T(8,128)S(1)} %fusion.57), channel_id=1, source_target_pairs={{48,112},{49,113},{50,114},{51,115},{52,116},{53,117},{54,118},{55... | collective-permute-start | bytes 98312 | tf_op jit(solution)/shard_map/ppermute | solution.py:72
  469.0 15.4 %collective-permute-start.12 = (f32[64,128]{1,0:T(8,128)S(1)}, f32[64,128]{1,0:T(8,128)S(1)}, u32[]{:S(2)}, u32[]{:S(2)}) collective-permute-start(f32[64,128]{1,0:T(8,128)S(1)} %fusion.51), channel_id=1, source_target_pairs={{16,32},{80,96},{17,33},{81,97},{18,34},{82,98},{19,35},{83,99},{2... | collective-permute-start | bytes 98312 | tf_op jit(solution)/shard_map/ppermute | solution.py:72
  477.7 6.7 %collective-permute-start.11 = (f32[64,128]{1,0:T(8,128)S(1)}, f32[64,128]{1,0:T(8,128)S(1)}, u32[]{:S(2)}, u32[]{:S(2)}) collective-permute-start(f32[64,128]{1,0:T(8,128)S(1)} %convolution_bitcast_fusion.7), channel_id=1, source_target_pairs={{16,0},{80,64},{17,1},{81,65},{18,2},{82,66},{19,3},{83,67},{20,4}... | collective-permute-start | bytes 98312 | tf_op jit(solution)/shard_map/ppermute | solution.py:72
  483.8 11.5 %collective-permute-start.16 = (f32[64,128]{1,0:T(8,128)S(1)}, f32[64,128]{1,0:T(8,128)S(1)}, u32[]{:S(2)}, u32[]{:S(2)}) collective-permute-start(f32[64,128]{1,0:T(8,128)S(1)} %add.51), channel_id=1, source_target_pairs={{48,16},{112,80},{49,17},{113,81},{50,18},{114,82},{51,19},{115,83... | collective-permute-start | bytes 98312 | tf_op jit(solution)/shard_map/ppermute | solution.py:72
  484.5 12.1 %collective-permute-start.13 = (f32[64,128]{1,0:T(8,128)S(1)}, f32[64,128]{1,0:T(8,128)S(1)}, u32[]{:S(2)}, u32[]{:S(2)}) collective-permute-start(f32[64,128]{1,0:T(8,128)S(1)} %add.50), channel_id=1, source_target_pairs={{0,1},{1,0},{2,3},{3,2},{4,5},{5,4},{6,7},{7,6},{8,9},{9,8},{10,11... | collective-permute-start | bytes 98312 | tf_op jit(solution)/shard_map/ppermute | solution.py:20
  495.3 28.5 %collective-permute-start.17 = (f32[64,128]{1,0:T(8,128)S(1)}, f32[64,128]{1,0:T(8,128)S(1)}, u32[]{:S(2)}, u32[]{:S(2)}) collective-permute-start(f32[64,128]{1,0:T(8,128)S(1)} %add.52), channel_id=1, source_target_pairs={{48,32},{16,0},{112,96},{80,64},{49,33},{17,1},{113,97},{81,65},{5... | collective-permute-start | bytes 98312 | tf_op jit(solution)/shard_map/ppermute | solution.py:72
  514.6 18.6 %collective-permute-start.14 = (f32[64,128]{1,0:T(8,128)S(1)}, f32[64,128]{1,0:T(8,128)S(1)}, u32[]{:S(2)}, u32[]{:S(2)}) collective-permute-start(f32[64,128]{1,0:T(8,128)S(1)} %fusion.54), channel_id=1, source_target_pairs={{0,16},{32,48},{64,80},{96,112},{1,17},{33,49},{65,81},{97,113},{2... | collective-permute-start | bytes 98312 | tf_op jit(solution)/shard_map/ppermute | solution.py:72
  550.7 5.8 collective-permute-start.18
  (24 other events, 529.1 us)
Sparse Core Ops, SparseCore 0:
  217.0 80.1 all-gather.2
